TPU v7x, 128 devices: a whole 4x4x4 slice. The times are simulated.
128 devices in a mesh: row: 8 (over x_lo, y), col: 16 (over x_hi, z, core).
Axes of the slice: x: 4 (x_hi: 2, x_lo: 2; x = x_hi * 2 + x_lo), y: 4, z: 4, core: 2. Of those that a mesh axis runs over, the one named last changes fastest.
Arguments:
- r_vector: bfloat16 [3072, 18432], P(('row', 'col')), may hold values from -100 to 100, as said below
- r_previous: bfloat16 [3072, 18432], P(('row', 'col')), may hold values from -100 to 100, as said below
- cycle_block: bfloat16 [18432, 18432], P('row', 'col'), may hold values from -0.046875 to 0.046875
- ladder_block: bfloat16 [48, 48, 48, 48], P(None, 'col', None, 'row'), may hold values from -0.125 to 0.125
- occ_energy: float32 [48], replicated, may hold values from -3 to -0.5
- vir_energy: float32 [384], replicated, may hold values from 0.3 to 4
- beta_previous: float32 [64], replicated, may hold values from 0.3 to 3
Outputs:
- next_vector: bfloat16 [3072, 18432], P(('row', 'col'))
- alpha_coef: float32 [64], replicated
- beta_coef: float32 [64], replicated
Inputs may be any that keep to these rules, and one draw needn't show every extreme that they name: `r_vector`: real-valued amplitudes, rough from entry to entry. `r_previous`: real-valued amplitudes, rough from entry to entry.
All inputs are finite; a program needn't handle non-finite values.
Results may differ from a plain program's by a relative error of at most 0.001.
Values may be sent and summed in bfloat16 or wider, within the bound.
A program may use at most 128 MiB of HBM per device.

v0:
```python
import jax
import jax.numpy as jnp
from jax import lax
from jax.sharding import PartitionSpec as P

O = 48
V = 384
NVEC = 64


def on_device(
    r_vector, r_previous, cycle_block, ladder_block, occ_energy, vir_energy, beta_previous
):
    n_row = lax.axis_size("row")
    n_col = lax.axis_size("col")
    local_rows = r_vector.shape[0]
    row_width = r_vector.shape[1]
    all_rows = NVEC * O
    j_part = ladder_block.shape[1]
    q_part = ladder_block.shape[3]
    column_part = lax.all_to_all(r_vector, "row", split_axis=1, concat_axis=0, tiled=True)
    shaped = column_part.reshape(n_row, 1, local_rows, column_part.shape[1])
    gathered = lax.all_gather(shaped, "col", axis=1, tiled=True)
    operand = gathered.reshape(all_rows, column_part.shape[1])
    cycle_part = jnp.dot(operand, cycle_block, preferred_element_type=jnp.float32)
    ladder_part = jnp.einsum(
        "ijpq,npqa->nija",
        ladder_block,
        operand.reshape(NVEC, O, q_part, V),
        preferred_element_type=jnp.float32,
    )
    out_width = j_part * V
    partial_value = cycle_part + ladder_part.reshape(all_rows, out_width)
    summed = lax.psum_scatter(
        partial_value.reshape(n_row, n_col, local_rows, out_width),
        "row",
        scatter_dimension=0,
        tiled=True,
    )
    sigma_rows = lax.all_to_all(summed, "col", split_axis=1, concat_axis=3, tiled=True)
    sigma_rows = sigma_rows.reshape(local_rows, row_width)
    linear_index = lax.axis_index("row") * n_col + lax.axis_index("col")
    row_ids = linear_index * local_rows + jnp.arange(local_rows, dtype=jnp.int32)
    occ_index = row_ids % O
    vec_of_row = row_ids // O
    occ_rows = jnp.sum(
        jnp.where(occ_index[:, None] == jnp.arange(O)[None, :], occ_energy[None, :], 0.0), axis=1
    )
    r_float = r_vector.astype(jnp.float32)
    prev_float = r_previous.astype(jnp.float32)
    diagonal = vir_energy[None, None, :] - occ_rows[:, None, None] - occ_energy[None, :, None]
    sigma_rows = sigma_rows + (diagonal * r_float.reshape(local_rows, O, V)).reshape(
        local_rows, row_width
    )
    member = (vec_of_row[:, None] == jnp.arange(NVEC)[None, :]).astype(jnp.float32)
    count_all = O * O * V

    def per_vector(row_sums):
        return jnp.sum(member * row_sums[:, None], axis=0)

    def per_row(coefs):
        return jnp.sum(member * coefs[None, :], axis=1)

    rs_sum, rr_sum = lax.psum(
        (
            per_vector(jnp.sum(r_float * sigma_rows, axis=1)),
            per_vector(jnp.sum(r_float * r_float, axis=1)),
        ),
        ("row", "col"),
    )
    alpha_coef = rs_sum / count_all / (rr_sum / count_all + 1e-06)
    residual_vec = (
        sigma_rows
        - per_row(alpha_coef)[:, None] * r_float
        - per_row(beta_previous)[:, None] * prev_float
    )
    norm_sum = lax.psum(per_vector(jnp.sum(residual_vec * residual_vec, axis=1)), ("row", "col"))
    beta_coef = jnp.sqrt(norm_sum / count_all + 1e-06)
    next_vector = (residual_vec / per_row(beta_coef)[:, None]).astype(jnp.bfloat16)
    return (next_vector, alpha_coef, beta_coef)


def solution(mesh):
    placed = (
        P(("row", "col"), None),
        P(("row", "col"), None),
        P("row", "col"),
        P(None, "col", None, "row"),
        P(),
        P(),
        P(),
    )
    return jax.shard_map(
        on_device,
        mesh=mesh,
        in_specs=placed,
        out_specs=(P(("row", "col"), None), P(), P()),
        check_vma=False,
    )
```

profile of v0, /device:TPU:0, one launch (start us, length us, event | category | flops | bytes accessed | tf_op | source)
XLA Modules:
  0.0 713.9 jit_solution(3815246468868575005)
XLA Ops:
  7.2 1.3 copy.67
  8.5 19.4 %all_to_all.31 = bf16[24,8,2304]{2,0,1:T(8,128)(2,1)S(1)} all-to-all(bf16[24,8,2304]{2,0,1:T(8,128)(2,1)S(1)} %bitcast.48), channel_id=1, replica_groups=mesh['row'=8,'col'=16] {'row'}, dimensions={1} | all-to-all | bytes 1769472 | tf_op jit(solution)/shard_map/all_to_all | solution.py:21
  27.9 1.1 copy.44
  29.0 97.4 %all-gather.3.cloned.1.call-done = bf16[8,384,2304]{2,0,1:T(8,128)(2,1)} async-done(((bf16[8,24,2304]{2,0,1:T(8,128)(2,1)}), bf16[8,384,2304]{2,0,1:T(8,128)(2,1)}) %all-gather.3.cloned.1.call-update) | async-done | bytes 14155792 | tf_op jit(solution)/shard_map/all_gather | solution.py:23
  126.4 15.0 %copy.45 = bf16[8,384,2304]{2,1,0:T(8,128)(2,1)} copy(bf16[8,384,2304]{2,0,1:T(8,128)(2,1)} %all-gather.3.cloned.1.call-done) | data formatting | bytes 28311552 | tf_op jit(solution)/shard_map/all_gather | solution.py:23
  141.4 28.1 %reshape_reshape.3 = bf16[64,48,6,384]{3,2,1,0:T(8,128)(2,1)} reshape(bf16[8,384,2304]{2,1,0:T(8,128)(2,1)} %copy.45) | data formatting | bytes 28311552 | tf_op jit(solution)/shard_map/reshape;reshape | solution.py:29
  169.6 13.5 %fusion.2 = f32[64,48,3,384]{3,1,2,0:T(8,128)} fusion(bf16[64,48,6,384,1]{3,2,1,0,4:T(8,128)(2,1)} %bitcast.38, bf16[48,3,48,6]{2,0,3,1:T(8,128)(2,1)S(1)} %copy-done), kind=kOutput, calls=%fused_computation.3 | convolution fusion | flops 2038431744 | bytes 28394496 | tf_op jit(solution)/shard_map/ijpq,npqa->nija/dot_general | solution.py:26
  183.1 16.5 %copy.48 = f32[64,48,3,384]{3,2,1,0:T(4,128)S(1)} copy(f32[64,48,3,384]{3,1,2,0:T(8,128)} %fusion.2) | data formatting | bytes 28311552 | tf_op jit(solution)/shard_map/ijpq,npqa->nija/transpose | solution.py:26
  199.6 6.7 copy.58
  206.3 24.9 %convolution_add_fusion = f32[3072,1152]{1,0:T(8,128)} fusion(f32[3072,1152]{1,0:T(8,128)} %bitcast.44, bf16[3072,2304]{1,0:T(8,128)(2,1)S(1)} %bitcast.37, bf16[2304,1152]{1,0:T(8,128)(2,1)} %param.9), kind=kOutput, calls=%fused_computation.2 | convolution fusion | flops 16310992896 | bytes 47775744 | tf_op jit(solution)/shard_map/dot_general | solution.py:25
  231.2 11.5 %copy.49 = f32[8,16,24,1152]{3,2,0,1:T(8,128)} copy(f32[8,16,24,1152]{3,2,1,0:T(8,128)} %bitcast.43) | data formatting | bytes 28311552 | tf_op jit(solution)/shard_map/reshape | solution.py:35
  242.7 0.6 copy-done.8
  243.3 0.6 dynamic-slice
  243.9 289.5 %all-reduce.4.cloned.1.call-done = f32[8,16,24,1152]{3,2,0,1:T(8,128)} async-done(((f32[8,16,24,1152]{3,2,0,1:T(8,128)}), f32[8,16,24,1152]{3,2,0,1:T(8,128)}) %all-reduce.4.cloned.1.call-update) | async-done | bytes 14155792
  533.4 3.4 constant_dynamic-slice_fusion
  536.8 6.8 all-to-all-start.1
  543.7 0.2 select_reduce_fusion.6
  543.9 0.1 broadcast_subtract_fusion
  544.0 0.1 sub.51
  544.1 0.6 copy.60
  544.7 24.7 %all-to-all-done.1 = f32[1,16,24,1152]{3,2,0,1:T(8,128)} async-done(((f32[1,16,24,1152]{3,2,0,1:T(8,128)}), f32[1,16,24,1152]{3,2,0,1:T(8,128)}, u32[]{:S(2)}, u32[]{:S(2)}) %all-to-all-start.1) | async-done | bytes 1769504 | tf_op jit(solution)/shard_map/all_to_all | solution.py:40
  569.5 1.7 copy.59
  571.2 1.2 copy-done.2
  572.4 0.8 fusion.6
  573.2 0.1 select_reduce_fusion.5
  573.3 64.4 %all-reduce.1 = (f32[64]{0:T(128)S(1)}, f32[64]{0:T(128)S(1)}) all-reduce(f32[64]{0:T(128)S(1)} %get-tuple-element.8, f32[64]{0:T(128)S(1)} %get-tuple-element.7), channel_id=1, replica_groups=mesh['row'=8,'col'=16] {'row','col'}, use_global_device_ids=true, to_apply=%region_7.8 | all-reduce | flops 128 | bytes 1024 | tf_op jit(solution)/shard_map/psum | solution.py:64
  637.8 0.2 select_reduce_fusion.3
  637.9 3.8 multiply_reduce_fusion
  641.8 0.1 select_reduce_fusion.1
  641.9 62.4 %psum.23 = f32[64]{0:T(128)S(1)} all-reduce(f32[64]{0:T(128)S(1)} %select_reduce_fusion.1), channel_id=1, replica_groups=mesh['row'=8,'col'=16] {'row','col'}, use_global_device_ids=true, to_apply=%region_12.13 | all-reduce | flops 64 | bytes 512 | tf_op jit(solution)/shard_map/psum | solution.py:77
  704.3 0.2 select_reduce_fusion
  704.5 2.6 divide_convert_fusion
  (36 shorter events, 0.3 us)
Async XLA Ops:
  7.2 162.4 %copy-start = (bf16[48,3,48,6]{2,0,3,1:T(8,128)(2,1)S(1)}, bf16[48,3,48,6]{2,0,3,1:T(8,128)(2,1)}, u32[]{:S(2)}) copy-start(bf16[48,3,48,6]{2,0,3,1:T(8,128)(2,1)} %param.10) | copy-start | bytes 248836
  7.2 119.2 %all-gather.3.cloned.1.call-start = ((), (), s32[]{:S(2)}) async-start(), calls=%async_computation.2 | async-start | bytes 15040512 | tf_op jit(solution)/shard_map/all_gather | solution.py:23
  29.0 504.4 %all-reduce.4.cloned.1.call-start = ((), (), s32[]{:S(2)}) async-start(), calls=%async_computation.3 | async-start | bytes 28311552
  183.1 23.2 %slice-start = ((s8[14155776]{0:T(1024)(128)(4,1)}), s8[4194304]{0:T(1024)(128)(4,1)S(1)}, s32[]{:S(2)}) async-start(s8[14155776]{0:T(1024)(128)(4,1)} %bitcast.35), calls=%async_computation.4 | async-start | bytes 8388608
  183.1 23.2 %slice-start.1 = ((s8[14155776]{0:T(1024)(128)(4,1)}), s8[4194304]{0:T(1024)(128)(4,1)S(1)}, s32[]{:S(2)}) async-start(s8[14155776]{0:T(1024)(128)(4,1)} %bitcast.35), calls=%async_computation.5 | async-start | bytes 8388608
  199.6 6.7 slice-start.2
  199.6 6.7 slice-start.3
  242.6 0.7 copy-start.8
  536.8 6.9 copy-start.5
  536.8 7.1 copy-start.4
  536.8 32.7 %all-to-all-start.1 = ((f32[1,16,24,1152]{3,2,0,1:T(8,128)}), f32[1,16,24,1152]{3,2,0,1:T(8,128)}, u32[]{:S(2)}, u32[]{:S(2)}) async-start(f32[1,16,24,1152]{3,2,0,1:T(8,128)} %constant_dynamic-slice_fusion), calls=%async_computation.1 | async-start | bytes 3538944 | tf_op jit(solution)/shard_map/all_to_all | solution.py:40
  569.5 2.9 copy-start.3
  571.2 1.2 copy-start.2
  572.4 65.3 %copy-start.6 = (f32[64]{0:T(128)S(1)}, f32[64]{0:T(128)}, u32[]{:S(2)}) copy-start(f32[64]{0:T(128)} %param.13) | copy-start | bytes 772
  637.7 4.0 copy-start.7
  637.9 69.1 %copy-start.1 = (bf16[48,3,48,6]{2,0,3,1:T(8,128)(2,1)S(1)}, bf16[48,3,48,6]{2,0,3,1:T(8,128)(2,1)}, u32[]{:S(2)}) copy-start(bf16[48,3,48,6]{2,0,3,1:T(8,128)(2,1)} %param.10) | copy-start | bytes 248836
  704.3 2.8 copy-start.9
Sparse Core Ops, SparseCore 0:
  29.1 97.2 all-gather.2
  242.8 290.5 all-reduce.3
where the time goes:
time: 716 us; the launch traced here: 714 us
  waiting for transfers between devices  412 us (58%)
  blocking collectives  146 us (20%)
  local copies, waits for them, and re-layouts  88.4 us (12%)
  matrix products  38.4 us (5%)
  between operations  14.2 us (2%)
  other arithmetic  8.03 us (1%)
    unnamed x3, waiting for transfers between devices  290 us
    all_gather x1, waiting for transfers between devices, on_device(): gathered = lax.all_gather(shaped, 'col', axis=1, tiled=True)  97.4 us
    psum x1, blocking collectives, on_device(): lax.psum((per_vector(jnp.sum(r_float * sigma_rows, axis=1)), per_vector(j...  64.4 us
    psum x1, blocking collectives, on_device(): lax.psum(per_vector(jnp.sum(residual_vec * residual_vec, axis=1)), ('row'...  62.4 us
    another operation x1, local copies, waits for them, and re-layouts, on_device(): operand.reshape(NVEC, O, q_part, V)  28.1 us
    dot_general x1, matrix products, on_device(): jnp.dot(operand, cycle_block, preferred_element_type=jnp.float32)  24.9 us
    all_to_all x1, waiting for transfers between devices, on_device(): lax.all_to_all(summed, 'col', split_axis=1, concat_axis=3, tiled=True)  24.7 us
    all_to_all x1, blocking collectives, on_device(): lax.all_to_all(r_vector, 'row', split_axis=1, concat_axis=0, tiled=True)  19.4 us
  transfers between devices with their start and end apart: 3, of which 3 were waited for; matrix products, arithmetic and copies ran while one was open for 0% of the time, Pallas kernels for 0%

commit v1 on v0

v1 whole, which is shorter than its diff:
```python
import functools

import jax
import jax.numpy as jnp
from jax import lax
from jax.experimental import pallas as pl
from jax.experimental.pallas import tpu as pltpu
from jax.sharding import PartitionSpec as P

O = 48
V = 384
NVEC = 64
COUNT = O * O * V
H = 1152
HALF = O // 2
MESH = pl.DeviceIdType.MESH
ORDER = ((0, 0), (0, 1), (0, 3), (1, 0), (0, 2), (1, 1), (1, 3), (1, 2))
FORWARD = {
    0: (("down", (0, 1), 1), ("up", (0, 1), 2), ("across", (0, 1), 3)),
    1: (("down", (0,), 4),),
    2: (("up", (1,), 4),),
    3: (("down", (0, 1), 5), ("up", (0, 1), 6)),
    4: (),
    5: (("down", (0,), 7),),
    6: (("up", (1,), 7),),
    7: (),
}
SLOT = {}
for _t in range(8):
    for _kind, _parts, _to in FORWARD[_t]:
        for _p in _parts:
            SLOT[(_t, _kind, _p)] = len(SLOT)
F32 = jnp.float32
BF16 = jnp.bfloat16


def kernel(
    r_ref, prev_hbm, c_hbm, w_ref, dcol_ref, occ_ref, bprev_ref,
    nxt_ref, g_ref,
    c_v, prev_v, sib, r48, ob, p, ra, tin, xin, sig, st_out, st_in,
    load_sem, sib_s, sib_r, pa_s, pa_r, ag_s, ag_r, hs_s, hs_r,
    a_s, a_r, b_s, b_r, x_s, x_r, f_s, f_r, st_s, st_r, g_s, g_r,
):
    row, col = lax.axis_index("row"), lax.axis_index("col")
    xl, y = row // 4, row % 4
    xh, z, core = col // 8, (col % 8) // 2, col % 2

    def dev(xl_=None, y_=None, xh_=None, z_=None, core_=None):
        a = xl if xl_ is None else xl_
        b = y if y_ is None else y_
        c = xh if xh_ is None else xh_
        d = z if z_ is None else z_
        e = core if core_ is None else core_
        return (a * 4 + b, c * 8 + d * 2 + e)

    def remote(src, dst, ssem, rsem, to):
        return pltpu.make_async_remote_copy(
            src_ref=src, dst_ref=dst, send_sem=ssem, recv_sem=rsem,
            device_id=to, device_id_type=MESH,
        )

    y1, y2, y3 = (y + 1) % 4, (y + 2) % 4, (y + 3) % 4
    up, down = dev(z_=(z + 1) % 4), dev(z_=(z + 3) % 4)
    across = dev(xh_=1 - xh)
    sibling = dev(core_=1 - core)
    target = {"up": up, "down": down, "across": across}

    load_c = pltpu.make_async_copy(c_hbm, c_v, load_sem.at[0])
    load_p = pltpu.make_async_copy(prev_hbm, prev_v, load_sem.at[1])
    load_c.start()
    load_p.start()

    barrier = pltpu.get_barrier_semaphore()
    for d in range(1, 8):
        pl.semaphore_signal(barrier, inc=1, device_id=((row + d) % 8, col), device_id_type=MESH)
    for d in range(1, 16):
        pl.semaphore_signal(barrier, inc=1, device_id=(row, (col + d) % 16), device_id_type=MESH)
    pl.semaphore_signal(barrier, inc=1, device_id=dev(xl_=1 - xl, xh_=1 - xh), device_id_type=MESH)
    pl.semaphore_wait(barrier, 23)

    def rel(d):
        yd, xd = (y + d % 4) % 4, (xl + d // 4) % 2
        return yd, xd

    def cols(yd, xd, half):
        return pl.ds(pl.multiple_of(((xd * 4 + yd) * 2 + half) * H, 128), H)

    rel_order = (6, 2, 5, 7, 1, 3, 4, 0)

    def swap(d):
        yd, xd = rel(d)
        return remote(r_ref.at[:, cols(yd, xd, 1 - core)], sib.at[d], sib_s.at[d], sib_r.at[d], sibling)

    blk0 = xh * 4 + z

    def exchange(d):
        yd, xd = rel(d)
        return remote(r48.at[d], ob.at[blk0, core, y, xl], pa_s.at[d], pa_r.at[d], dev(xl_=xd, y_=yd))

    for d in rel_order:
        swap(d).start()
    for d in rel_order:
        yd, xd = rel(d)
        swap(d).wait_recv()
        mine = r_ref[:, cols(yd, xd, core)].astype(F32)
        other = sib[d].astype(F32)
        first = jnp.where(core == 0, mine, other)
        second = jnp.where(core == 0, other, mine)
        both = jnp.concatenate([first, second], axis=0).astype(BF16)
        if d == 0:
            ob[blk0, core, y, xl] = both
        else:
            r48[d] = both
            exchange(d).start()

    def block_of(t):
        out_x, out_z = xh, z
        for k, (dx, dz) in enumerate(ORDER):
            out_x = jnp.where(t == k, (xh + dx) % 2, out_x)
            out_z = jnp.where(t == k, (z + dz) % 4, out_z)
        return out_x, out_z

    def forward(t, kind, part, to):
        dx, dz = ORDER[t]
        blk = ((xh + dx) % 2) * 4 + (z + dz) % 4
        piece = ob.at[blk, core, pl.ds(2 * part, 2)]
        return remote(piece, piece, ag_s.at[SLOT[(t, kind, part)]], ag_r.at[to, part], target[kind])

    def hand(t):
        bx, bz = block_of(t)
        piece = ob.at[bx * 4 + bz, core]
        return remote(piece, piece, hs_s.at[t], hs_r.at[t], sibling)

    def landed(t, part):
        bx, bz = block_of(t)
        piece = ob.at[bx * 4 + bz, core, pl.ds(2 * part, 2)]
        return remote(piece, piece, ag_s.at[0], ag_r.at[t, part], sibling)

    def sibling_landed(t):
        bx, bz = block_of(t)
        piece = ob.at[bx * 4 + bz, 1 - core]
        return remote(piece, piece, hs_s.at[t], hs_r.at[t], sibling)

    def first_hop(s, side):
        to = dev(y_=y1) if side == 0 else dev(y_=y3)
        return remote(p.at[s, y2, side], ra.at[s, side], a_s.at[s, side], a_r.at[s, side], to)

    def second_hop(s, side):
        yd = y1 if side == 0 else y3
        return remote(p.at[s, yd], tin.at[s, side], b_s.at[s, side], b_r.at[s, side], dev(y_=yd))

    def beside(s):
        return remote(p.at[s, y, 1 - xl], xin.at[s], x_s.at[s], x_r.at[s], dev(xl_=1 - xl))

    def home(s, core_to):
        bx, bz = block_of(s)
        return remote(
            p.at[s, y, xl, pl.ds(core_to * HALF, HALF)], sig.at[col],
            f_s.at[s, core_to], f_r.at[col], dev(xh_=bx, z_=bz, core_=core_to),
        )

    def home_sibling():
        return remote(
            p.at[0, y, xl, pl.ds(pl.multiple_of((1 - core) * HALF, 8), HALF)], sig.at[col],
            f_s.at[0, 0], f_r.at[col], sibling,
        )

    load_c.wait()

    def step(t, carry):
        @pl.when(t == 0)
        def _():
            for d in range(1, 8):
                exchange(d).wait_recv()

        @pl.when(jnp.logical_and(t > 0, t < 8))
        def _():
            landed(t, 0).wait_recv()
            landed(t, 1).wait_recv()

        for k in range(8):
            if FORWARD[k]:
                @pl.when(t == k)
                def _(k=k):
                    for kind, parts, to in FORWARD[k]:
                        for part in parts:
                            forward(k, kind, part, to).start()

        @pl.when(t < 8)
        def _():
            hand(t).start()
            sibling_landed(t).wait_recv()
            bx, bz = block_of(t)
            blk = bx * 4 + bz
            x0 = ob[blk, 0].reshape(8 * O, H)
            x1 = ob[blk, 1].reshape(8 * O, H)
            acc = jnp.dot(x0, c_v[:H], preferred_element_type=F32)
            acc = acc + jnp.dot(x1, c_v[H:], preferred_element_type=F32)
            p[t] = acc.reshape(4, 2, O, H)

            def ladder(v, carry2):
                vy, vx = v // 2, v % 2
                stack = jnp.concatenate(
                    [ob[blk, h, vy, vx, :, q * V:(q + 1) * V] for h in range(2) for q in range(3)],
                    axis=0,
                )
                part = jnp.dot(w_ref[...], stack, preferred_element_type=F32)
                for j in range(3):
                    p[t, vy, vx, :, j * V:(j + 1) * V] += part[j * O:(j + 1) * O]
                return carry2

            lax.fori_loop(0, 8, ladder, 0)
            first_hop(t, 0).start()
            first_hop(t, 1).start()

        @pl.when(jnp.logical_and(t >= 1, t <= 8))
        def _():
            s = t - 1
            first_hop(s, 0).wait_recv()
            p[s, y1, 0] += ra[s, 0]
            second_hop(s, 0).start()
            first_hop(s, 1).wait_recv()
            p[s, y3, 1] += ra[s, 1]
            second_hop(s, 1).start()

        @pl.when(jnp.logical_and(t >= 2, t <= 9))
        def _():
            s = t - 2
            second_hop(s, 0).wait_recv()
            second_hop(s, 1).wait_recv()
            p[s, y, 1 - xl] += tin[s, 0, 1 - xl] + tin[s, 1, 1 - xl]
            beside(s).start()
            p[s, y, xl] += tin[s, 0, xl] + tin[s, 1, xl]

        @pl.when(t >= 3)
        def _():
            s = t - 3
            beside(s).wait_recv()
            p[s, y, xl] += xin[s]

            @pl.when(s == 0)
            def _():
                home_sibling().start()
                sig[col] = p[0, y, xl, pl.ds(pl.multiple_of(core * HALF, 8), HALF)]

            @pl.when(s > 0)
            def _():
                home(s, 0).start()
                home(s, 1).start()

        return carry

    lax.fori_loop(0, 11, step, 0)
    load_p.wait()

    def sums(val):
        total = val[:, 0:128]
        for k in range(1, H // 128):
            total = total + val[:, k * 128:(k + 1) * 128]
        return total[0:8] + total[8:16] + total[16:24]

    occ_col = occ_ref[:, 0:1]

    def arrived(d):
        from_col = (col + d) % 16
        return remote(sig.at[from_col], sig.at[from_col], f_s.at[0, 0], f_r.at[from_col], sibling)

    def first_pass(d, carry):
        acc_s, acc_r = carry
        @pl.when(d > 0)
        def _():
            arrived(d).wait_recv()
        k = (col + d) % 16
        rv = r_ref[:, pl.ds(pl.multiple_of(k * H, 128), H)].astype(F32)
        val = sig[k] + (dcol_ref[k] - occ_col) * rv
        sig[k] = val
        return acc_s + sums(rv * val), acc_r + sums(rv * rv)

    zero = jnp.zeros((8, 128), F32)
    acc_s, acc_r = lax.fori_loop(0, 16, first_pass, (zero, zero))
    line = lax.broadcasted_iota(jnp.int32, (8, 128), 0)

    def pair(k):
        return remote(st_out.at[k], st_in.at[k], st_s.at[k], st_r.at[k], sibling)

    st_out[0] = jnp.where(line == 0, jnp.sum(acc_s), jnp.sum(acc_r))
    pair(0).start()
    pair(0).wait_recv()
    both = st_out[0] + st_in[0]
    alpha = both[0:1] / COUNT / (both[1:2] / COUNT + 1e-06)
    alpha_1 = alpha[:, 0:1]
    bprev_1 = bprev_ref[0:1, 0:1]

    def second_pass(k, acc):
        at = pl.ds(pl.multiple_of(k * H, 128), H)
        val = sig[k] - alpha_1 * r_ref[:, at].astype(F32) - bprev_1 * prev_v[:, at].astype(F32)
        sig[k] = val
        return acc + sums(val * val)

    acc_n = lax.fori_loop(0, 16, second_pass, zero)
    st_out[1] = jnp.where(line == 0, jnp.sum(acc_n), 0.0)
    pair(1).start()
    pair(1).wait_recv()
    norm = (st_out[1] + st_in[1])[0:1]
    beta = jnp.sqrt(norm / COUNT + 1e-06)
    inv = (1.0 / beta)[:, 0:1]

    g_ref[xl, y, xh, z] = jnp.where(line == 0, alpha, beta)

    def spread(axis, d):
        if axis == 0:
            piece, to = g_ref.at[xl, y, xh, z], dev(z_=(z + d) % 4)
        elif axis == 1:
            piece, to = g_ref.at[xl, y, xh], dev(y_=(y + d) % 4)
        else:
            piece = g_ref.at[xl, :, xh]
            to = dev(xl_=(xl + d % 2) % 2, xh_=(xh + d // 2) % 2)
        return remote(piece, piece, g_s.at[axis, d - 1], g_r.at[axis, d - 1], to)

    for d in range(1, 4):
        spread(0, d).start()

    def third_pass(k, carry):
        nxt_ref[:, pl.ds(pl.multiple_of(k * H, 128), H)] = (sig[k] * inv).astype(BF16)
        return carry

    lax.fori_loop(0, 16, third_pass, 0)
    for axis in range(3):
        for d in range(1, 4):
            if axis:
                spread(axis, d).start()
        for d in range(1, 4):
            spread(axis, d).wait_recv()

    for d in range(8):
        swap(d).wait_send()
        if d:
            exchange(d).wait_send()
    for k in range(8):
        for kind, parts, to in FORWARD[k]:
            for part in parts:
                forward(k, kind, part, to).wait_send()

    def drain(s, carry):
        hand(s).wait_send()
        for side in range(2):
            first_hop(s, side).wait_send()
            second_hop(s, side).wait_send()
        beside(s).wait_send()
        return carry

    lax.fori_loop(0, 8, drain, 0)
    home_sibling().wait_send()

    def drain_home(s, carry):
        home(s, 0).wait_send()
        home(s, 1).wait_send()
        return carry

    lax.fori_loop(1, 8, drain_home, 0)
    pair(0).wait_send()
    pair(1).wait_send()
    for axis in range(3):
        for d in range(1, 4):
            spread(axis, d).wait_send()


def on_device(
    r_vector, r_previous, cycle_block, ladder_block, occ_energy, vir_energy, beta_previous
):
    row, col = lax.axis_index("row"), lax.axis_index("col")
    core = col % 2
    weights = jnp.transpose(ladder_block, (1, 0, 3, 2)).reshape(3 * O, 6 * O)
    dcol = (vir_energy[None, :] - occ_energy[:, None]).reshape(16, 1, H)
    occ_rows = lax.dynamic_slice(occ_energy, (core * HALF,), (HALF,))
    occ_rows = jnp.broadcast_to(occ_rows[:, None], (HALF, 128))
    mine = lax.dynamic_slice(beta_previous, (row * 8 + col // 2,), (1,))
    bprev = jnp.broadcast_to(mine[:, None], (8, 128))
    vmem, hbm = pl.BlockSpec(memory_space=pltpu.VMEM), pl.BlockSpec(memory_space=pl.ANY)
    dma = pltpu.SemaphoreType.DMA
    nxt, spread = pl.pallas_call(
        kernel,
        out_shape=(
            jax.ShapeDtypeStruct((HALF, O * V), BF16),
            jax.ShapeDtypeStruct((2, 4, 2, 4, 8, 128), F32),
        ),
        in_specs=[vmem, hbm, hbm, vmem, vmem, vmem, vmem],
        out_specs=(vmem, vmem),
        scratch_shapes=[
            pltpu.VMEM((2 * H, H), BF16),
            pltpu.VMEM((HALF, O * V), BF16),
            pltpu.VMEM((8, HALF, H), BF16),
            pltpu.VMEM((8, O, H), BF16),
            pltpu.VMEM((8, 2, 4, 2, O, H), BF16),
            pltpu.VMEM((8, 4, 2, O, H), F32),
            pltpu.VMEM((8, 2, O, H), F32),
            pltpu.VMEM((8, 2, 2, O, H), F32),
            pltpu.VMEM((8, O, H), F32),
            pltpu.VMEM((16, HALF, H), F32),
            pltpu.VMEM((2, 8, 128), F32),
            pltpu.VMEM((2, 8, 128), F32),
            dma((2,)), dma((8,)), dma((8,)), dma((8,)), dma((8,)),
            dma((len(SLOT),)), dma((8, 2)), dma((8,)), dma((8,)),
            dma((8, 2)), dma((8, 2)), dma((8, 2)), dma((8, 2)),
            dma((8,)), dma((8,)), dma((8, 2)), dma((16,)),
            dma((2,)), dma((2,)), dma((3, 3)), dma((3, 3)),
        ],
        compiler_params=pltpu.CompilerParams(
            collective_id=0, has_side_effects=True, vmem_limit_bytes=66 * 1024 * 1024 - 2 * 1024 * 1024 - 65536,
        ),
        name="sigma_step",
    )(r_vector, r_previous, cycle_block, weights, dcol, occ_rows, bprev)
    spread = spread.reshape(NVEC, 8, 128)
    return (nxt, spread[:, 0, 0], spread[:, 1, 0])


def solution(mesh):
    placed = (
        P(("row", "col"), None),
        P(("row", "col"), None),
        P("row", "col"),
        P(None, "col", None, "row"),
        P(),
        P(),
        P(),
    )
    return jax.shard_map(
        on_device,
        mesh=mesh,
        in_specs=placed,
        out_specs=(P(("row", "col"), None), P(), P()),
        check_vma=False,
    )
```

time: 716 us -> 211 us (0.29)
  waiting for transfers between devices: 412 us -> 0 us
  Pallas kernels: 0 us -> 198 us
  blocking collectives: 146 us -> 0 us
  local copies, waits for them, and re-layouts: 88.4 us -> 11.7 us
  matrix products: 38.4 us -> 0 us
  between operations: 14.2 us -> 0.69 us
  other arithmetic: 8.03 us -> 0.68 us
    unnamed x3 -> x0, waiting for transfers between devices: 290 us -> none
    pallas_call x0 -> x1, Pallas kernels: none -> 198 us  [on_device(): pl.pallas_call(kernel, out_shape=(jax.ShapeDtypeStruct((HALF, O * V), BF1...]
    psum x2 -> x0, blocking collectives: 127 us -> none  [the longest x1 64.4 us: on_device(): lax.psum((per_vector(jnp.sum(r_float * sigma_rows, axis=1)), per_vector(j...]
    all_gather x1 -> x0, waiting for transfers between devices: 97.4 us -> none  [on_device(): gathered = lax.all_gather(shaped, 'col', axis=1, tiled=True)]
    dot_general x2 -> x0, matrix products: 38.4 us -> none  [the longest x1 24.9 us: on_device(): jnp.dot(operand, cycle_block, preferred_element_type=jnp.float32)]
    another operation x1 -> x0, local copies, waits for them, and re-layouts: 28.1 us -> none  [on_device(): operand.reshape(NVEC, O, q_part, V)]
    all_to_all x1 -> x0, waiting for transfers between devices: 24.7 us -> none  [on_device(): lax.all_to_all(summed, 'col', split_axis=1, concat_axis=3, tiled=True)]
    all_to_all x1 -> x0, blocking collectives: 19.4 us -> none  [on_device(): lax.all_to_all(r_vector, 'row', split_axis=1, concat_axis=0, tiled=True)]
  transfers between devices with their start and end apart: 3 -> 0, of which waited for: 3 -> 0; matrix products, arithmetic and copies ran while one was open for 0% -> 0% of each run, Pallas kernels for 0% -> 0%
where the time goes in v1:
time: 211 us
  Pallas kernels  198 us (94%)
  local copies, waits for them, and re-layouts  11.7 us (6%)
    pallas_call x1, Pallas kernels, on_device(): pl.pallas_call(kernel, out_shape=(jax.ShapeDtypeStruct((HALF, O * V), BF1...  198 us

profile of v1, /device:TPU:0, one launch (start us, length us, event | category | flops | bytes accessed | tf_op | source)
XLA Modules:
  0.0 210.9 jit_solution(50236929298385025)
XLA Ops:
  0.7 0.7 dynamic_slice.6
  1.4 1.2 dynamic_slice.7
  2.6 1.2 broadcast_in_dim.8.bprev_ref
  3.9 0.7 sub.32
  4.6 0.7 sub.35
  5.3 0.7 broadcast_in_dim.6.occ_ref
  6.0 0.1 sub.36
  6.1 0.1 sub.40
  6.2 0.7 broadcast_subtract_fusion.dcol_ref
  6.8 1.0 copy.17
  7.9 0.8 reshape.56.w_ref
  8.7 197.8 %sigma_step.1 = (bf16[24,18432]{1,0:T(8,128)(2,1)}, f32[2,4,2,4,8,128]{5,4,3,2,1,0:T(8,128)}) custom-call(bf16[24,18432]{1,0:T(8,128)(2,1)} %r_ref.1, bf16[24,18432]{1,0:T(8,128)(2,1)} %prev_hbm.1, bf16[2304,1152]{1,0:T(8,128)(2,1)} %c_hbm.1, bf16[144,288]{1,0:T(8,128)(2,1)} %reshape.56.w_ref, f32[16,1,1152]{2,1,0:T(1,128)} %broadcast_subtract_fusion.dcol_ref, ...), custom_call_target="tpu_custom_call" | custom-call | tf_op jit(solution)/shard_map/sigma_step/pallas_call | solution.py:381
  206.5 1.1 fusion
  207.6 0.6 copy.23
  208.2 0.6 copy.22
  208.8 2.1 %copy.25 = bf16[24,18432]{1,0:T(8,128)(2,1)} copy(bf16[24,18432]{1,0:T(8,128)(2,1)} %get-tuple-element.12) | data formatting | bytes 1769472
  (1 shorter events, 0.0 us)

commit v2 on v1

--- a/solution.py
+++ b/solution.py
@@ -32,12 +32,54 @@
             SLOT[(_t, _kind, _p)] = len(SLOT)
 F32 = jnp.float32
 BF16 = jnp.bfloat16
+TILES = 37
+LEVELS = 32600.0
+BIG = 12582912.0
+
+
+def nearest(x):
+    return (x + BIG) - BIG
+
+
+def encode(src, dst):
+    top = jnp.abs(src[:, 0:128])
+    for k in range(1, H // 128):
+        top = jnp.maximum(top, jnp.abs(src[:, k * 128:(k + 1) * 128]))
+    peak = jnp.maximum(jnp.max(top), 1e-30)
+    unit = jnp.full((8, 128), peak, F32) * (1.0 / LEVELS)
+    dst[TILES - 1] = unit
+    scale = 1.0 / unit
+    for i in range(O // 8):
+        rows = slice(i * 8, i * 8 + 8)
+        for k in range(3):
+            q = [nearest(src[rows, j * V + k * 128:j * V + k * 128 + 128] * scale) for j in range(3)]
+            high = nearest(q[2] * (1.0 / 256.0))
+            low = q[2] - high * 256.0
+            dst[i * 3 + k] = q[0] * 512.0 + high
+            dst[18 + i * 3 + k] = q[1] * 512.0 + low
+
+
+def decode_add(msgs, dst):
+    units = [m[TILES - 1] for m in msgs]
+    for i in range(O // 8):
+        rows = slice(i * 8, i * 8 + 8)
+        for k in range(3):
+            at = [slice(j * V + k * 128, j * V + k * 128 + 128) for j in range(3)]
+            total = [dst[rows, a] for a in at]
+            for m, unit in zip(msgs, units):
+                one, two = m[i * 3 + k], m[18 + i * 3 + k]
+                qa = nearest(one * (1.0 / 512.0))
+                qb = nearest(two * (1.0 / 512.0))
+                qc = (one - qa * 512.0) * 256.0 + (two - qb * 512.0)
+                total = [t + v * unit for t, v in zip(total, (qa, qb, qc))]
+            for a, t in zip(at, total):
+                dst[rows, a] = t
 
 
 def kernel(
-    r_ref, prev_hbm, c_hbm, w_ref, dcol_ref, occ_ref, bprev_ref,
+    r_ref, prev_hbm, c_hbm, w_ref, vir_ref, occ_ref, bprev_ref,
     nxt_ref, g_ref,
-    c_v, prev_v, sib, r48, ob, p, ra, tin, xin, sig, st_out, st_in,
+    c_v, prev_v, sib, r48, ob, p, ao, ra, bo, tin, xo, xin, sig, st_out, st_in,
     load_sem, sib_s, sib_r, pa_s, pa_r, ag_s, ag_r, hs_s, hs_r,
     a_s, a_r, b_s, b_r, x_s, x_r, f_s, f_r, st_s, st_r, g_s, g_r,
 ):
@@ -143,14 +185,17 @@
 
     def first_hop(s, side):
         to = dev(y_=y1) if side == 0 else dev(y_=y3)
-        return remote(p.at[s, y2, side], ra.at[s, side], a_s.at[s, side], a_r.at[s, side], to)
-
-    def second_hop(s, side):
+        return remote(ao.at[s, side], ra.at[s, side], a_s.at[s, side], a_r.at[s, side], to)
+
+    def second_hop(s, side, which):
         yd = y1 if side == 0 else y3
-        return remote(p.at[s, yd], tin.at[s, side], b_s.at[s, side], b_r.at[s, side], dev(y_=yd))
+        return remote(
+            bo.at[s, side, which], tin.at[s, side, which],
+            b_s.at[s, side, which], b_r.at[s, side, which], dev(y_=yd),
+        )
 
     def beside(s):
-        return remote(p.at[s, y, 1 - xl], xin.at[s], x_s.at[s], x_r.at[s], dev(xl_=1 - xl))
+        return remote(xo.at[s], xin.at[s], x_s.at[s], x_r.at[s], dev(xl_=1 - xl))
 
     def home(s, core_to):
         bx, bz = block_of(s)
@@ -167,7 +212,44 @@
 
     load_c.wait()
 
+    def relay(s):
+        for side in range(2):
+            first_hop(s, side).wait_recv()
+            share = p.at[s, y1 if side == 0 else y3, side]
+            decode_add([ra.at[s, side]], share)
+            encode(share, bo.at[s, side, side])
+            second_hop(s, side, side).start()
+
+    def across_pair(s):
+        for side in range(2):
+            for which in range(2):
+                second_hop(s, side, which).wait_recv()
+        decode_add([tin.at[s, 0, 1 - xl], tin.at[s, 1, 1 - xl]], p.at[s, y, 1 - xl])
+        encode(p.at[s, y, 1 - xl], xo.at[s])
+        beside(s).start()
+        decode_add([tin.at[s, 0, xl], tin.at[s, 1, xl]], p.at[s, y, xl])
+
+    def deliver(s):
+        beside(s).wait_recv()
+        decode_add([xin.at[s]], p.at[s, y, xl])
+
+        @pl.when(s == 0)
+        def _():
+            home_sibling().start()
+            sig[col] = p[0, y, xl, pl.ds(pl.multiple_of(core * HALF, 8), HALF)]
+
+        @pl.when(s > 0)
+        def _():
+            home(s, 0).start()
+            home(s, 1).start()
+
     def step(t, carry):
+        @pl.when(t == 1)
+        def _():
+            relay(t - 1)
+            across_pair(t - 1)
+            deliver(t - 1)
+
         @pl.when(t == 0)
         def _():
             for d in range(1, 8):
@@ -210,43 +292,24 @@
                 return carry2
 
             lax.fori_loop(0, 8, ladder, 0)
-            first_hop(t, 0).start()
-            first_hop(t, 1).start()
-
-        @pl.when(jnp.logical_and(t >= 1, t <= 8))
-        def _():
-            s = t - 1
-            first_hop(s, 0).wait_recv()
-            p[s, y1, 0] += ra[s, 0]
-            second_hop(s, 0).start()
-            first_hop(s, 1).wait_recv()
-            p[s, y3, 1] += ra[s, 1]
-            second_hop(s, 1).start()
-
-        @pl.when(jnp.logical_and(t >= 2, t <= 9))
-        def _():
-            s = t - 2
-            second_hop(s, 0).wait_recv()
-            second_hop(s, 1).wait_recv()
-            p[s, y, 1 - xl] += tin[s, 0, 1 - xl] + tin[s, 1, 1 - xl]
-            beside(s).start()
-            p[s, y, xl] += tin[s, 0, xl] + tin[s, 1, xl]
-
-        @pl.when(t >= 3)
-        def _():
-            s = t - 3
-            beside(s).wait_recv()
-            p[s, y, xl] += xin[s]
-
-            @pl.when(s == 0)
-            def _():
-                home_sibling().start()
-                sig[col] = p[0, y, xl, pl.ds(pl.multiple_of(core * HALF, 8), HALF)]
-
-            @pl.when(s > 0)
-            def _():
-                home(s, 0).start()
-                home(s, 1).start()
+            for side in range(2):
+                encode(p.at[t, y2, side], ao.at[t, side])
+                first_hop(t, side).start()
+            for side in range(2):
+                encode(p.at[t, y1 if side == 0 else y3, 1 - side], bo.at[t, side, 1 - side])
+                second_hop(t, side, 1 - side).start()
+
+        @pl.when(jnp.logical_and(t >= 2, t <= 8))
+        def _():
+            relay(t - 1)
+
+        @pl.when(jnp.logical_and(t >= 3, t <= 9))
+        def _():
+            across_pair(t - 2)
+
+        @pl.when(t >= 4)
+        def _():
+            deliver(t - 3)
 
         return carry
 
@@ -259,7 +322,12 @@
             total = total + val[:, k * 128:(k + 1) * 128]
         return total[0:8] + total[8:16] + total[16:24]
 
-    occ_col = occ_ref[:, 0:1]
+    line24 = lax.broadcasted_iota(jnp.int32, (HALF, 128), 0)
+    occ_mat = jnp.zeros((HALF, 128), F32)
+    for i in range(HALF):
+        occ_mat = jnp.where(line24 == i, occ_ref[core * HALF + i], occ_mat)
+    occ_col = occ_mat[:, 0:1]
+    vir_row = vir_ref[...]
 
     def arrived(d):
         from_col = (col + d) % 16
@@ -272,7 +340,8 @@
             arrived(d).wait_recv()
         k = (col + d) % 16
         rv = r_ref[:, pl.ds(pl.multiple_of(k * H, 128), H)].astype(F32)
-        val = sig[k] + (dcol_ref[k] - occ_col) * rv
+        levels = jnp.concatenate([vir_row - occ_ref[k * 3 + j] for j in range(3)], axis=1)
+        val = sig[k] + (levels - occ_col) * rv
         sig[k] = val
         return acc_s + sums(rv * val), acc_r + sums(rv * rv)
 
@@ -289,7 +358,7 @@
     both = st_out[0] + st_in[0]
     alpha = both[0:1] / COUNT / (both[1:2] / COUNT + 1e-06)
     alpha_1 = alpha[:, 0:1]
-    bprev_1 = bprev_ref[0:1, 0:1]
+    bprev_1 = bprev_ref[row * 8 + xh * 4 + z]
 
     def second_pass(k, acc):
         at = pl.ds(pl.multiple_of(k * H, 128), H)
@@ -345,7 +414,8 @@
         hand(s).wait_send()
         for side in range(2):
             first_hop(s, side).wait_send()
-            second_hop(s, side).wait_send()
+            second_hop(s, side, 0).wait_send()
+            second_hop(s, side, 1).wait_send()
         beside(s).wait_send()
         return carry
 
@@ -368,15 +438,9 @@
 def on_device(
     r_vector, r_previous, cycle_block, ladder_block, occ_energy, vir_energy, beta_previous
 ):
-    row, col = lax.axis_index("row"), lax.axis_index("col")
-    core = col % 2
     weights = jnp.transpose(ladder_block, (1, 0, 3, 2)).reshape(3 * O, 6 * O)
-    dcol = (vir_energy[None, :] - occ_energy[:, None]).reshape(16, 1, H)
-    occ_rows = lax.dynamic_slice(occ_energy, (core * HALF,), (HALF,))
-    occ_rows = jnp.broadcast_to(occ_rows[:, None], (HALF, 128))
-    mine = lax.dynamic_slice(beta_previous, (row * 8 + col // 2,), (1,))
-    bprev = jnp.broadcast_to(mine[:, None], (8, 128))
     vmem, hbm = pl.BlockSpec(memory_space=pltpu.VMEM), pl.BlockSpec(memory_space=pl.ANY)
+    smem = pl.BlockSpec(memory_space=pltpu.SMEM)
     dma = pltpu.SemaphoreType.DMA
     nxt, spread = pl.pallas_call(
         kernel,
@@ -384,7 +448,7 @@
             jax.ShapeDtypeStruct((HALF, O * V), BF16),
             jax.ShapeDtypeStruct((2, 4, 2, 4, 8, 128), F32),
         ),
-        in_specs=[vmem, hbm, hbm, vmem, vmem, vmem, vmem],
+        in_specs=[vmem, hbm, hbm, vmem, vmem, smem, smem],
         out_specs=(vmem, vmem),
         scratch_shapes=[
             pltpu.VMEM((2 * H, H), BF16),
@@ -393,15 +457,18 @@
             pltpu.VMEM((8, O, H), BF16),
             pltpu.VMEM((8, 2, 4, 2, O, H), BF16),
             pltpu.VMEM((8, 4, 2, O, H), F32),
-            pltpu.VMEM((8, 2, O, H), F32),
-            pltpu.VMEM((8, 2, 2, O, H), F32),
-            pltpu.VMEM((8, O, H), F32),
+            pltpu.VMEM((8, 2, TILES, 8, 128), F32),
+            pltpu.VMEM((8, 2, TILES, 8, 128), F32),
+            pltpu.VMEM((8, 2, 2, TILES, 8, 128), F32),
+            pltpu.VMEM((8, 2, 2, TILES, 8, 128), F32),
+            pltpu.VMEM((8, TILES, 8, 128), F32),
+            pltpu.VMEM((8, TILES, 8, 128), F32),
             pltpu.VMEM((16, HALF, H), F32),
             pltpu.VMEM((2, 8, 128), F32),
             pltpu.VMEM((2, 8, 128), F32),
             dma((2,)), dma((8,)), dma((8,)), dma((8,)), dma((8,)),
             dma((len(SLOT),)), dma((8, 2)), dma((8,)), dma((8,)),
-            dma((8, 2)), dma((8, 2)), dma((8, 2)), dma((8, 2)),
+            dma((8, 2)), dma((8, 2)), dma((8, 2, 2)), dma((8, 2, 2)),
             dma((8,)), dma((8,)), dma((8, 2)), dma((16,)),
             dma((2,)), dma((2,)), dma((3, 3)), dma((3, 3)),
         ],
@@ -409,7 +476,7 @@
             collective_id=0, has_side_effects=True, vmem_limit_bytes=66 * 1024 * 1024 - 2 * 1024 * 1024 - 65536,
         ),
         name="sigma_step",
-    )(r_vector, r_previous, cycle_block, weights, dcol, occ_rows, bprev)
+    )(r_vector, r_previous, cycle_block, weights, vir_energy.reshape(1, V), occ_energy, beta_previous)
     spread = spread.reshape(NVEC, 8, 128)
     return (nxt, spread[:, 0, 0], spread[:, 1, 0])
 

time: 211 us -> 175 us (0.83)
  Pallas kernels: 198 us -> 167 us
  local copies, waits for them, and re-layouts: 11.7 us -> 7.48 us
    pallas_call x1, Pallas kernels: 198 us -> 167 us  [on_device(): pl.pallas_call(kernel, out_shape=(jax.ShapeDtypeStruct((HALF, O * V), BF1...]
where the time goes in v2:
time: 175 us
  Pallas kernels  167 us (95%)
  local copies, waits for them, and re-layouts  7.48 us (4%)
    pallas_call x1, Pallas kernels, on_device(): pl.pallas_call(kernel, out_shape=(jax.ShapeDtypeStruct((HALF, O * V), BF1...  167 us

profile of v2, /device:TPU:0, one launch (start us, length us, event | category | flops | bytes accessed | tf_op | source)
XLA Modules:
  0.0 175.0 jit_solution(2591762754678620179)
XLA Ops:
  0.6 1.0 copy.13
  1.6 0.8 reshape.15.w_ref
  2.5 1.3 reshape.16.vir_ref
  3.7 166.9 %sigma_step.1 = (bf16[24,18432]{1,0:T(8,128)(2,1)}, f32[2,4,2,4,8,128]{5,4,3,2,1,0:T(8,128)}) custom-call(bf16[24,18432]{1,0:T(8,128)(2,1)} %r_ref.1, bf16[24,18432]{1,0:T(8,128)(2,1)} %prev_hbm.1, bf16[2304,1152]{1,0:T(8,128)(2,1)} %c_hbm.1, bf16[144,288]{1,0:T(8,128)(2,1)} %reshape.15.w_ref, f32[1,384]{1,0:T(1,128)} %reshape.16.vir_ref, f32[48]{0:T(128)} %occ_ref.1, ...), custom_call_target="tpu_custom_call" | custom-call | tf_op jit(solution)/shard_map/sigma_step/pallas_call | solution.py:445
  170.6 1.1 fusion
  171.7 0.6 copy.16
  172.3 0.6 copy.17
  172.9 2.1 %copy.19 = bf16[24,18432]{1,0:T(8,128)(2,1)} copy(bf16[24,18432]{1,0:T(8,128)(2,1)} %get-tuple-element.12) | data formatting | bytes 1769472

commit v3 on v2

v3 whole, which is shorter than its diff:
```python
import functools

import jax
import jax.numpy as jnp
from jax import lax
from jax.experimental import pallas as pl
from jax.experimental.pallas import tpu as pltpu
from jax.sharding import PartitionSpec as P

O = 48
V = 384
NVEC = 64
COUNT = O * O * V
H = 1152
HALF = O // 2
MESH = pl.DeviceIdType.MESH
ORDER = ((0, 0), (0, 1), (0, 3), (1, 0), (0, 2), (1, 1), (1, 3), (1, 2))
FORWARD = {
    1: (("down", (0,), 4),),
    2: (("up", (1,), 4),),
    3: (("down", (0, 1), 5), ("up", (0, 1), 6)),
    5: (("down", (0,), 7),),
    6: (("up", (1,), 7),),
}
SLOT = {}
for _t in FORWARD:
    for _kind, _parts, _to in FORWARD[_t]:
        for _p in _parts:
            SLOT[(_t, _kind, _p)] = len(SLOT)
FIRST = (("down", 1), ("up", 2), ("across", 3))
F32 = jnp.float32
BF16 = jnp.bfloat16
HALVES = (
    (0, 0), (0, 1), (1, 0), (3, 0), (3, 1), (2, 0), (1, 1), (6, 0),
    (6, 1), (2, 1), (5, 0), (5, 1), (7, 0), (7, 1), (4, 0), (4, 1),
)
ARRIVALS = (
    (), (), ((3, 0), (1, 0),), (), ((3, 1), (2, 1), (2, 0),), ((1, 1),), (), ((5, 0), (6, 0),),
    ((6, 1),), (), ((5, 1),), ((4, 0),), ((7, 1), (7, 0),), ((4, 1),), (), (),
)
ROWS = HALF // 8
TILES = 6 * ROWS + 1
LEVELS = 43000.0
SPAN = 384.0
BIG = 12582912.0


def nearest(x):
    return (x + BIG) - BIG


def encode(src, dst):
    top = jnp.abs(src[:, 0:128])
    for k in range(1, H // 128):
        top = jnp.maximum(top, jnp.abs(src[:, k * 128:(k + 1) * 128]))
    peak = jnp.maximum(jnp.max(top), 1e-30)
    unit = jnp.full((8, 128), peak, F32) * (1.0 / LEVELS)
    dst[TILES - 1] = unit
    scale = 1.0 / unit
    for i in range(ROWS):
        rows = slice(i * 8, i * 8 + 8)
        for k in range(3):
            q = [nearest(src[rows, j * V + k * 128:j * V + k * 128 + 128] * scale) for j in range(3)]
            high = nearest(q[2] * (1.0 / 256.0))
            low = q[2] - high * 256.0
            dst[i * 3 + k] = q[0] * SPAN + high
            dst[3 * ROWS + i * 3 + k] = q[1] * SPAN + low


def decode_add(msgs, dst):
    units = [m[TILES - 1] for m in msgs]
    for i in range(ROWS):
        rows = slice(i * 8, i * 8 + 8)
        for k in range(3):
            at = [slice(j * V + k * 128, j * V + k * 128 + 128) for j in range(3)]
            total = [dst[rows, a] for a in at]
            for m, unit in zip(msgs, units):
                one, two = m[i * 3 + k], m[3 * ROWS + i * 3 + k]
                qa = nearest(one * (1.0 / SPAN))
                qb = nearest(two * (1.0 / SPAN))
                qc = (one - qa * SPAN) * 256.0 + (two - qb * SPAN)
                total = [t + v * unit for t, v in zip(total, (qa, qb, qc))]
            for a, t in zip(at, total):
                dst[rows, a] = t


def kernel(
    r_hbm, prev_hbm, c_hbm, w_hbm, vir_ref, occ_ref, bprev_ref,
    nxt_ref, g_ref,
    r_ref, w_ref, c_v, prev_v, sib, r48, ob, p, ao, ra, bo, tin, xo, xin, sig, st_out, st_in, g_out, g_in,
    load_sem, sib_s, sib_r, pa_s, pa_r, v_s, ag_s, ag_r, hs_s, hs_r,
    a_s, a_r, b_s, b_r, x_s, x_r, f_s, f_r, st_s, st_r, g_s, g_r,
):
    row, col = lax.axis_index("row"), lax.axis_index("col")
    xl, y = row // 4, row % 4
    xh, z, core = col // 8, (col % 8) // 2, col % 2

    def dev(xl_=None, y_=None, xh_=None, z_=None, core_=None):
        a = xl if xl_ is None else xl_
        b = y if y_ is None else y_
        c = xh if xh_ is None else xh_
        d = z if z_ is None else z_
        e = core if core_ is None else core_
        return (a * 4 + b, c * 8 + d * 2 + e)

    def remote(src, dst, ssem, rsem, to):
        return pltpu.make_async_remote_copy(
            src_ref=src, dst_ref=dst, send_sem=ssem, recv_sem=rsem,
            device_id=to, device_id_type=MESH,
        )

    y1, y2, y3 = (y + 1) % 4, (y + 2) % 4, (y + 3) % 4
    up, down = dev(z_=(z + 1) % 4), dev(z_=(z + 3) % 4)
    across = dev(xh_=1 - xh)
    sibling = dev(core_=1 - core)
    target = {"up": up, "down": down, "across": across}

    barrier = pltpu.get_barrier_semaphore()
    for d in range(1, 8):
        pl.semaphore_signal(barrier, inc=1, device_id=((row + d) % 8, col), device_id_type=MESH)
    for d in range(1, 16):
        pl.semaphore_signal(barrier, inc=1, device_id=(row, (col + d) % 16), device_id_type=MESH)
    pl.semaphore_signal(barrier, inc=1, device_id=dev(xl_=1 - xl, xh_=1 - xh), device_id_type=MESH)
    load_r = pltpu.make_async_copy(r_hbm, r_ref, load_sem.at[2])
    load_w = pltpu.make_async_copy(w_hbm, w_ref, load_sem.at[3])
    load_r.start()
    load_c = pltpu.make_async_copy(c_hbm, c_v, load_sem.at[0])
    load_p = pltpu.make_async_copy(prev_hbm, prev_v, load_sem.at[1])
    load_c.start()
    load_p.start()
    load_w.start()
    load_r.wait()
    pl.semaphore_wait(barrier, 23)

    def rel(d):
        yd, xd = (y + d % 4) % 4, (xl + d // 4) % 2
        return yd, xd

    def cols(yd, xd, half):
        return pl.ds(pl.multiple_of(((xd * 4 + yd) * 2 + half) * H, 128), H)

    near, far = (1, 3, 2), (4, 5, 7, 6)

    def swap(d):
        yd, xd = rel(d)
        return remote(r_ref.at[:, cols(yd, xd, 1 - core)], sib.at[d], sib_s.at[d], sib_r.at[d], sibling)

    blk0 = xh * 4 + z

    def exchange(d):
        yd, xd = rel(d)
        return remote(r48.at[d], ob.at[blk0, core, xl, y], pa_s.at[d], pa_r.at[d], dev(xl_=xd, y_=yd))

    def pass_on(d, to):
        kind, block = FIRST[to]
        ys, xs = (y + 4 - d % 4) % 4, (xl + d // 4) % 2
        piece = ob.at[blk0, core, xs, ys]
        return remote(piece, piece, v_s.at[to, d], ag_r.at[block, d // 4], target[kind])

    for d in (0,) + near + far:
        swap(d).start()
    for d in (0,) + near + far:
        yd, xd = rel(d)
        swap(d).wait_recv()
        mine = r_ref[:, cols(yd, xd, core)].astype(F32)
        other = sib[d].astype(F32)
        first = jnp.where(core == 0, mine, other)
        second = jnp.where(core == 0, other, mine)
        both = jnp.concatenate([first, second], axis=0).astype(BF16)
        if d == 0:
            ob[blk0, core, xl, y] = both
        else:
            r48[d] = both
            exchange(d).start()
    for to in range(3):
        pass_on(0, to).start()
    for d in near:
        exchange(d).wait_recv()
        for to in range(3):
            pass_on(d, to).start()

    def block_of(t):
        out_x, out_z = xh, z
        for k, (dx, dz) in enumerate(ORDER):
            out_x = jnp.where(t == k, (xh + dx) % 2, out_x)
            out_z = jnp.where(t == k, (z + dz) % 4, out_z)
        return out_x, out_z

    def forward(t, kind, part, to):
        dx, dz = ORDER[t]
        blk = ((xh + dx) % 2) * 4 + (z + dz) % 4
        piece = ob.at[blk, core, (part + xl) % 2]
        return remote(piece, piece, ag_s.at[SLOT[(t, kind, part)]], ag_r.at[to, part], target[kind])

    def hand(t, part):
        bx, bz = block_of(t)
        piece = ob.at[bx * 4 + bz, core, (part + xl) % 2]
        return remote(piece, piece, hs_s.at[t, part], hs_r.at[t, part], sibling)

    def landed(t, part):
        bx, bz = block_of(t)
        piece = ob.at[bx * 4 + bz, core, (part + xl) % 2]
        return remote(piece, piece, ag_s.at[0], ag_r.at[t, part], sibling)

    def sibling_landed(t, part):
        bx, bz = block_of(t)
        piece = ob.at[bx * 4 + bz, 1 - core, (part + xl) % 2]
        return remote(piece, piece, hs_s.at[t, part], hs_r.at[t, part], sibling)

    def half_of(u):
        t, g, keep = jnp.int32(0), jnp.int32(0), jnp.int32(0)
        for k, (bt, bg) in enumerate(HALVES):
            t, g = jnp.where(u == k, bt, t), jnp.where(u == k, bg, g)
            keep = jnp.where(u == k, HALVES.index((bt, 0)), keep)
        return t, g, keep

    def first_hop(s, side):
        to = dev(y_=y1) if side == 0 else dev(y_=y3)
        return remote(ao.at[s, side], ra.at[s, side], a_s.at[s, side], a_r.at[s, side], to)

    def second_hop(s, side, which):
        yd = y1 if side == 0 else y3
        return remote(
            bo.at[s, side, which], tin.at[s, side, which],
            b_s.at[s, side, which], b_r.at[s, side, which], dev(y_=yd),
        )

    def beside(t):
        return remote(xo.at[t], xin.at[t], x_s.at[t], x_r.at[t], dev(xl_=1 - xl))

    def home(t, keep, core_to):
        bx, bz = block_of(t)
        return remote(
            p.at[keep, y, pl.ds(core_to * HALF, HALF)], sig.at[col],
            f_s.at[t, core_to], f_r.at[col], dev(xh_=bx, z_=bz, core_=core_to),
        )

    def home_sibling():
        return remote(
            p.at[0, y, pl.ds(pl.multiple_of((1 - core) * HALF, 8), HALF)], sig.at[col],
            f_s.at[0, 0], f_r.at[col], sibling,
        )

    load_c.wait()
    load_w.wait()

    rows_of = (slice(0, HALF), slice(HALF, O))

    def relay(u):
        for side in range(2):
            first_hop(u, side).wait_recv()
            share = p.at[u, y1 if side == 0 else y3, rows_of[side]]
            decode_add([ra.at[u, side]], share)
            encode(share, bo.at[u, side, side])
            second_hop(u, side, side).start()

    def across_pair(u):
        t, g, _ = half_of(u)
        for which in range(2):
            second_hop(u, 0, which).wait_recv()
            second_hop(u, 1, which).wait_recv()
            decode_add([tin.at[u, 0, which], tin.at[u, 1, which]], p.at[u, y, rows_of[which]])

        @pl.when(g == 1)
        def _():
            for which in range(2):
                encode(p.at[u, y, rows_of[which]], xo.at[t, which])
            beside(t).start()

    def deliver(u):
        t, g, keep = half_of(u)

        @pl.when(g == 1)
        def _():
            beside(t).wait_recv()
            for which in range(2):
                decode_add([xin.at[t, which]], p.at[keep, y, rows_of[which]])

            @pl.when(t == 0)
            def _():
                home_sibling().start()
                sig[col] = p[0, y, pl.ds(pl.multiple_of(core * HALF, 8), HALF)]

            @pl.when(t > 0)
            def _():
                home(t, keep, 0).start()
                home(t, keep, 1).start()

    def step(u, carry):
        t, g, _ = half_of(u)

        @pl.when(u == 1)
        def _():
            for d in far:
                exchange(d).wait_recv()
                for to in range(3):
                    pass_on(d, to).start()

        @pl.when(u < 2)
        def _():
            hand(0, u).start()

        for k, todo in enumerate(ARRIVALS):
            if todo:
                @pl.when(u == k)
                def _(todo=todo):
                    for bt, part in todo:
                        landed(bt, part).wait_recv()
                        for kind, parts, to in FORWARD.get(bt, ()):
                            if part in parts:
                                forward(bt, kind, part, to).start()
                        hand(bt, part).start()

        @pl.when(u < 16)
        def _():
            sibling_landed(t, g).wait_recv()
            bx, bz = block_of(t)
            h = (g + xl) % 2
            blk = bx * 4 + bz
            x0 = ob[blk, 0, h].reshape(4 * O, H)
            x1 = ob[blk, 1, h].reshape(4 * O, H)
            acc = jnp.dot(x0, c_v[:H], preferred_element_type=F32)
            acc = acc + jnp.dot(x1, c_v[H:], preferred_element_type=F32)
            p[u] = acc.reshape(4, O, H)

            def ladder(v, carry2):
                stack = jnp.concatenate(
                    [ob[blk, w, h, v, :, q * V:(q + 1) * V] for w in range(2) for q in range(3)],
                    axis=0,
                )
                part = jnp.dot(w_ref[...], stack, preferred_element_type=F32)
                for j in range(3):
                    p[u, v, :, j * V:(j + 1) * V] += part[j * O:(j + 1) * O]
                return carry2

            lax.fori_loop(0, 4, ladder, 0)
            for side in range(2):
                encode(p.at[u, y2, rows_of[side]], ao.at[u, side])
                first_hop(u, side).start()
            for side in range(2):
                encode(p.at[u, y1 if side == 0 else y3, rows_of[1 - side]], bo.at[u, side, 1 - side])
                second_hop(u, side, 1 - side).start()

        @pl.when(jnp.logical_and(u >= 1, u <= 16))
        def _():
            relay(u - 1)

        @pl.when(jnp.logical_and(u >= 2, u <= 17))
        def _():
            across_pair(u - 2)

        @pl.when(u >= 3)
        def _():
            deliver(u - 3)

        return carry

    lax.fori_loop(0, 19, step, 0)
    load_p.wait()

    def sums(val):
        total = val[:, 0:128]
        for k in range(1, H // 128):
            total = total + val[:, k * 128:(k + 1) * 128]
        return total[0:8] + total[8:16] + total[16:24]

    line24 = lax.broadcasted_iota(jnp.int32, (HALF, 128), 0)
    occ_mat = jnp.zeros((HALF, 128), F32)
    for i in range(HALF):
        occ_mat = jnp.where(line24 == i, occ_ref[core * HALF + i], occ_mat)
    occ_col = occ_mat[:, 0:1]
    vir_row = vir_ref[...].reshape(1, V)

    def arrived(d):
        from_col = (col + d) % 16
        return remote(sig.at[from_col], sig.at[from_col], f_s.at[0, 0], f_r.at[from_col], sibling)

    def first_pass(d, carry):
        acc_s, acc_r = carry
        @pl.when(d > 0)
        def _():
            arrived(d).wait_recv()
        k = (col + d) % 16
        rv = r_ref[:, pl.ds(pl.multiple_of(k * H, 128), H)].astype(F32)
        levels = jnp.concatenate([vir_row - occ_ref[k * 3 + j] for j in range(3)], axis=1)
        val = sig[k] + (levels - occ_col) * rv
        sig[k] = val
        return acc_s + sums(rv * val), acc_r + sums(rv * rv)

    zero = jnp.zeros((8, 128), F32)
    acc_s, acc_r = lax.fori_loop(0, 16, first_pass, (zero, zero))
    line = lax.broadcasted_iota(jnp.int32, (8, 128), 0)

    def pair(k):
        return remote(st_out.at[k], st_in.at[k], st_s.at[k], st_r.at[k], sibling)

    st_out[0] = jnp.where(line == 0, jnp.sum(acc_s), jnp.sum(acc_r))
    pair(0).start()
    pair(0).wait_recv()
    both = st_out[0] + st_in[0]
    alpha = both[0:1] / COUNT / (both[1:2] / COUNT + 1e-06)
    alpha_1 = alpha[:, 0:1]
    bprev_1 = bprev_ref[row * 8 + xh * 4 + z]

    def second_pass(k, acc):
        at = pl.ds(pl.multiple_of(k * H, 128), H)
        val = sig[k] - alpha_1 * r_ref[:, at].astype(F32) - bprev_1 * prev_v[:, at].astype(F32)
        sig[k] = val
        return acc + sums(val * val)

    acc_n = lax.fori_loop(0, 16, second_pass, zero)
    st_out[1] = jnp.where(line == 0, jnp.sum(acc_n), 0.0)
    pair(1).start()
    pair(1).wait_recv()
    norm = (st_out[1] + st_in[1])[0:1]
    beta = jnp.sqrt(norm / COUNT + 1e-06)
    inv = (1.0 / beta)[:, 0:1]

    lane = lax.broadcasted_iota(jnp.int32, (8, 128), 1)
    vec = row * 8 + xh * 4 + z
    g_out[0] = jnp.where(lane == vec, jnp.where(line == 0, alpha, beta), 0.0)

    def spread(axis, d):
        if axis == 0:
            to = dev(z_=(z + d) % 4)
        elif axis == 1:
            to = dev(y_=(y + d) % 4)
        else:
            to = dev(xl_=(xl + d % 2) % 2, xh_=(xh + d // 2) % 2)
        return remote(g_out.at[axis], g_in.at[axis, d - 1], g_s.at[axis, d - 1], g_r.at[axis, d - 1], to)

    for d in range(1, 4):
        spread(0, d).start()

    def third_pass(k, carry):
        nxt_ref[:, pl.ds(pl.multiple_of(k * H, 128), H)] = (sig[k] * inv).astype(BF16)
        return carry

    lax.fori_loop(0, 16, third_pass, 0)
    for axis in range(3):
        for d in range(1, 4):
            spread(axis, d).wait_recv()
        merged = g_out[axis] + g_in[axis, 0] + g_in[axis, 1] + g_in[axis, 2]
        if axis == 2:
            g_ref[...] = merged
        else:
            g_out[axis + 1] = merged
            for d in range(1, 4):
                spread(axis + 1, d).start()

    for d in range(8):
        swap(d).wait_send()
        if d:
            exchange(d).wait_send()
        for to in range(3):
            pass_on(d, to).wait_send()
    for bt in FORWARD:
        for kind, parts, to in FORWARD[bt]:
            for part in parts:
                forward(bt, kind, part, to).wait_send()

    def drain(u, carry):
        t, g, keep = half_of(u)
        hand(t, g).wait_send()
        for side in range(2):
            first_hop(u, side).wait_send()
            second_hop(u, side, 0).wait_send()
            second_hop(u, side, 1).wait_send()

        @pl.when(g == 1)
        def _():
            beside(t).wait_send()

            @pl.when(t == 0)
            def _():
                home_sibling().wait_send()

            @pl.when(t > 0)
            def _():
                home(t, keep, 0).wait_send()
                home(t, keep, 1).wait_send()

        return carry

    lax.fori_loop(0, 16, drain, 0)
    pair(0).wait_send()
    pair(1).wait_send()
    for axis in range(3):
        for d in range(1, 4):
            spread(axis, d).wait_send()


def on_device(
    r_vector, r_previous, cycle_block, ladder_block, occ_energy, vir_energy, beta_previous
):
    weights = jnp.transpose(ladder_block, (1, 0, 3, 2)).reshape(3 * O, 6 * O)
    vmem, hbm = pl.BlockSpec(memory_space=pltpu.VMEM), pl.BlockSpec(memory_space=pl.ANY)
    smem = pl.BlockSpec(memory_space=pltpu.SMEM)
    dma = pltpu.SemaphoreType.DMA
    nxt, spread = pl.pallas_call(
        kernel,
        out_shape=(
            jax.ShapeDtypeStruct((HALF, O * V), BF16),
            jax.ShapeDtypeStruct((8, 128), F32),
        ),
        in_specs=[hbm, hbm, hbm, hbm, vmem, smem, smem],
        out_specs=(vmem, vmem),
        scratch_shapes=[
            pltpu.VMEM((HALF, O * V), BF16),
            pltpu.VMEM((3 * O, 6 * O), BF16),
            pltpu.VMEM((2 * H, H), BF16),
            pltpu.VMEM((HALF, O * V), BF16),
            pltpu.VMEM((8, HALF, H), BF16),
            pltpu.VMEM((8, O, H), BF16),
            pltpu.VMEM((8, 2, 2, 4, O, H), BF16),
            pltpu.VMEM((16, 4, O, H), F32),
            pltpu.VMEM((16, 2, TILES, 8, 128), F32),
            pltpu.VMEM((16, 2, TILES, 8, 128), F32),
            pltpu.VMEM((16, 2, 2, TILES, 8, 128), F32),
            pltpu.VMEM((16, 2, 2, TILES, 8, 128), F32),
            pltpu.VMEM((8, 2, TILES, 8, 128), F32),
            pltpu.VMEM((8, 2, TILES, 8, 128), F32),
            pltpu.VMEM((16, HALF, H), F32),
            pltpu.VMEM((2, 8, 128), F32),
            pltpu.VMEM((2, 8, 128), F32),
            pltpu.VMEM((3, 8, 128), F32),
            pltpu.VMEM((3, 3, 8, 128), F32),
            dma((4,)), dma((8,)), dma((8,)), dma((8,)), dma((8,)), dma((3, 8)),
            dma((len(SLOT),)), dma((8, 2)), dma((8, 2)), dma((8, 2)),
            dma((16, 2)), dma((16, 2)), dma((16, 2, 2)), dma((16, 2, 2)),
            dma((8,)), dma((8,)), dma((8, 2)), dma((16,)),
            dma((2,)), dma((2,)), dma((3, 3)), dma((3, 3)),
        ],
        compiler_params=pltpu.CompilerParams(
            collective_id=0, has_side_effects=True, vmem_limit_bytes=66 * 1024 * 1024 - 2 * 1024 * 1024 - 65536,
        ),
        name="sigma_step",
    )(r_vector, r_previous, cycle_block, weights, vir_energy, occ_energy, beta_previous)
    return (nxt, spread[0, :NVEC], spread[1, :NVEC])


def solution(mesh):
    placed = (
        P(("row", "col"), None),
        P(("row", "col"), None),
        P("row", "col"),
        P(None, "col", None, "row"),
        P(),
        P(),
        P(),
    )
    return jax.shard_map(
        on_device,
        mesh=mesh,
        in_specs=placed,
        out_specs=(P(("row", "col"), None), P(), P()),
        check_vma=False,
    )
```

time: 175 us -> 159 us (0.909)
  Pallas kernels: 167 us -> 153 us
  local copies, waits for them, and re-layouts: 7.48 us -> 5.25 us
    pallas_call x1, Pallas kernels: 167 us -> 153 us  [on_device(): pl.pallas_call(kernel, out_shape=(jax.ShapeDtypeStruct((HALF, O * V), BF1...]
where the time goes in v3:
time: 159 us
  Pallas kernels  153 us (96%)
  local copies, waits for them, and re-layouts  5.25 us (3%)
    pallas_call x1, Pallas kernels, on_device(): pl.pallas_call(kernel, out_shape=(jax.ShapeDtypeStruct((HALF, O * V), BF1...  153 us

profile of v3, /device:TPU:0, one launch (start us, length us, event | category | flops | bytes accessed | tf_op | source)
XLA Modules:
  0.0 158.8 jit_solution(10414420047257888553)
XLA Ops:
  0.6 1.0 copy.11
  1.6 0.8 reshape.9.w_hbm
  2.5 152.9 %sigma_step.1 = (bf16[24,18432]{1,0:T(8,128)(2,1)}, f32[8,128]{1,0:T(8,128)}) custom-call(bf16[24,18432]{1,0:T(8,128)(2,1)} %r_hbm.1, bf16[24,18432]{1,0:T(8,128)(2,1)} %prev_hbm.1, bf16[2304,1152]{1,0:T(8,128)(2,1)} %c_hbm.1, bf16[144,288]{1,0:T(8,128)(2,1)} %reshape.9.w_hbm, f32[384]{0:T(512)} %vir_ref.1, f32[48]{0:T(128)} %occ_ref.1, f32[64]{0:T(128)} %bprev_ref.1), custom_call_target="tpu_custom_call" | custom-call | tf_op jit(solution)/shard_map/sigma_step/pallas_call | solution.py:500
  155.4 1.3 slice_bitcast_fusion
  156.6 2.1 %copy.13 = bf16[24,18432]{1,0:T(8,128)(2,1)} copy(bf16[24,18432]{1,0:T(8,128)(2,1)} %get-tuple-element.12) | data formatting | bytes 1769472

commit v4 on v3

--- a/solution.py
+++ b/solution.py
@@ -32,11 +32,11 @@
 BF16 = jnp.bfloat16
 HALVES = (
     (0, 0), (0, 1), (1, 0), (3, 0), (3, 1), (2, 0), (1, 1), (6, 0),
-    (6, 1), (2, 1), (5, 0), (5, 1), (7, 0), (7, 1), (4, 0), (4, 1),
+    (2, 1), (6, 1), (5, 0), (5, 1), (7, 0), (7, 1), (4, 0), (4, 1),
 )
 ARRIVALS = (
-    (), (), ((3, 0), (1, 0),), (), ((3, 1), (2, 1), (2, 0),), ((1, 1),), (), ((5, 0), (6, 0),),
-    ((6, 1),), (), ((5, 1),), ((4, 0),), ((7, 1), (7, 0),), ((4, 1),), (), (),
+    (), (), ((3, 0), (1, 0),), (), ((2, 0), (1, 1), (3, 1), (2, 1),), (), ((6, 0), (5, 0),), (),
+    ((4, 0),), ((6, 1),), ((5, 1),), (), ((7, 1), (4, 1), (7, 0),), (), (), (),
 )
 ROWS = HALF // 8
 TILES = 6 * ROWS + 1
@@ -84,10 +84,23 @@
                 dst[rows, a] = t
 
 
+def decode_set(msg, dst):
+    unit = msg[TILES - 1]
+    for i in range(ROWS):
+        rows = slice(i * 8, i * 8 + 8)
+        for k in range(3):
+            one, two = msg[i * 3 + k], msg[3 * ROWS + i * 3 + k]
+            qa = nearest(one * (1.0 / SPAN))
+            qb = nearest(two * (1.0 / SPAN))
+            qc = (one - qa * SPAN) * 256.0 + (two - qb * SPAN)
+            for j, v in enumerate((qa, qb, qc)):
+                dst[rows, j * V + k * 128:j * V + k * 128 + 128] = v * unit
+
+
 def kernel(
     r_hbm, prev_hbm, c_hbm, w_hbm, vir_ref, occ_ref, bprev_ref,
     nxt_ref, g_ref,
-    r_ref, w_ref, c_v, prev_v, sib, r48, ob, p, ao, ra, bo, tin, xo, xin, sig, st_out, st_in, g_out, g_in,
+    r_ref, w_ref, c_v, prev_v, sib, r48, ob, p, ao, ra, bo, tin, xo, xin, ho, hin, sig, st_out, st_in, g_out, g_in,
     load_sem, sib_s, sib_r, pa_s, pa_r, v_s, ag_s, ag_r, hs_s, hs_r,
     a_s, a_r, b_s, b_r, x_s, x_r, f_s, f_r, st_s, st_r, g_s, g_r,
 ):
@@ -159,7 +172,7 @@
 
     for d in (0,) + near + far:
         swap(d).start()
-    for d in (0,) + near + far:
+    def prepare(d):
         yd, xd = rel(d)
         swap(d).wait_recv()
         mine = r_ref[:, cols(yd, xd, core)].astype(F32)
@@ -172,6 +185,9 @@
         else:
             r48[d] = both
             exchange(d).start()
+
+    for d in (0, 2, 1, 3, 6, 5, 7, 4):
+        prepare(d)
     for to in range(3):
         pass_on(0, to).start()
     for d in near:
@@ -228,18 +244,15 @@
     def beside(t):
         return remote(xo.at[t], xin.at[t], x_s.at[t], x_r.at[t], dev(xl_=1 - xl))
 
-    def home(t, keep, core_to):
+    def home(t, core_to):
         bx, bz = block_of(t)
         return remote(
-            p.at[keep, y, pl.ds(core_to * HALF, HALF)], sig.at[col],
-            f_s.at[t, core_to], f_r.at[col], dev(xh_=bx, z_=bz, core_=core_to),
+            ho.at[t, core_to], hin.at[col], f_s.at[t, core_to], f_r.at[col],
+            dev(xh_=bx, z_=bz, core_=core_to),
         )
 
     def home_sibling():
-        return remote(
-            p.at[0, y, pl.ds(pl.multiple_of((1 - core) * HALF, 8), HALF)], sig.at[col],
-            f_s.at[0, 0], f_r.at[col], sibling,
-        )
+        return remote(ho.at[0, 0], hin.at[col], f_s.at[0, 0], f_r.at[col], sibling)
 
     load_c.wait()
     load_w.wait()
@@ -278,23 +291,18 @@
 
             @pl.when(t == 0)
             def _():
+                encode(p.at[0, y, pl.ds(pl.multiple_of((1 - core) * HALF, 8), HALF)], ho.at[0, 0])
                 home_sibling().start()
                 sig[col] = p[0, y, pl.ds(pl.multiple_of(core * HALF, 8), HALF)]
 
             @pl.when(t > 0)
             def _():
-                home(t, keep, 0).start()
-                home(t, keep, 1).start()
+                for which in range(2):
+                    encode(p.at[keep, y, rows_of[which]], ho.at[t, which])
+                    home(t, which).start()
 
     def step(u, carry):
         t, g, _ = half_of(u)
-
-        @pl.when(u == 1)
-        def _():
-            for d in far:
-                exchange(d).wait_recv()
-                for to in range(3):
-                    pass_on(d, to).start()
 
         @pl.when(u < 2)
         def _():
@@ -333,29 +341,39 @@
                     p[u, v, :, j * V:(j + 1) * V] += part[j * O:(j + 1) * O]
                 return carry2
 
-            lax.fori_loop(0, 4, ladder, 0)
+            @pl.when(u == 0)
+            def _():
+                for d in far:
+                    exchange(d).wait_recv()
+                    for to in range(3):
+                        pass_on(d, to).start()
+
+            ladder(y2, 0)
             for side in range(2):
                 encode(p.at[u, y2, rows_of[side]], ao.at[u, side])
                 first_hop(u, side).start()
             for side in range(2):
-                encode(p.at[u, y1 if side == 0 else y3, rows_of[1 - side]], bo.at[u, side, 1 - side])
+                yd = y1 if side == 0 else y3
+                ladder(yd, 0)
+                encode(p.at[u, yd, rows_of[1 - side]], bo.at[u, side, 1 - side])
                 second_hop(u, side, 1 - side).start()
+            ladder(y, 0)
 
         @pl.when(jnp.logical_and(u >= 1, u <= 16))
         def _():
             relay(u - 1)
 
-        @pl.when(jnp.logical_and(u >= 2, u <= 17))
-        def _():
-            across_pair(u - 2)
-
-        @pl.when(u >= 3)
-        def _():
-            deliver(u - 3)
+        @pl.when(jnp.logical_and(u >= 3, u <= 18))
+        def _():
+            across_pair(u - 3)
+
+        @pl.when(u >= 4)
+        def _():
+            deliver(u - 4)
 
         return carry
 
-    lax.fori_loop(0, 19, step, 0)
+    lax.fori_loop(0, 20, step, 0)
     load_p.wait()
 
     def sums(val):
@@ -373,13 +391,14 @@
 
     def arrived(d):
         from_col = (col + d) % 16
-        return remote(sig.at[from_col], sig.at[from_col], f_s.at[0, 0], f_r.at[from_col], sibling)
+        return remote(ho.at[0, 0], hin.at[from_col], f_s.at[0, 0], f_r.at[from_col], sibling)
 
     def first_pass(d, carry):
         acc_s, acc_r = carry
         @pl.when(d > 0)
         def _():
             arrived(d).wait_recv()
+            decode_set(hin.at[(col + d) % 16], sig.at[(col + d) % 16])
         k = (col + d) % 16
         rv = r_ref[:, pl.ds(pl.multiple_of(k * H, 128), H)].astype(F32)
         levels = jnp.concatenate([vir_row - occ_ref[k * 3 + j] for j in range(3)], axis=1)
@@ -477,8 +496,8 @@
 
             @pl.when(t > 0)
             def _():
-                home(t, keep, 0).wait_send()
-                home(t, keep, 1).wait_send()
+                home(t, 0).wait_send()
+                home(t, 1).wait_send()
 
         return carry
 
@@ -520,6 +539,8 @@
             pltpu.VMEM((16, 2, 2, TILES, 8, 128), F32),
             pltpu.VMEM((8, 2, TILES, 8, 128), F32),
             pltpu.VMEM((8, 2, TILES, 8, 128), F32),
+            pltpu.VMEM((8, 2, TILES, 8, 128), F32),
+            pltpu.VMEM((16, TILES, 8, 128), F32),
             pltpu.VMEM((16, HALF, H), F32),
             pltpu.VMEM((2, 8, 128), F32),
             pltpu.VMEM((2, 8, 128), F32),

time: 159 us -> 149 us (0.937)
  Pallas kernels: 153 us -> 143 us
    pallas_call x1, Pallas kernels: 153 us -> 143 us  [on_device(): pl.pallas_call(kernel, out_shape=(jax.ShapeDtypeStruct((HALF, O * V), BF1...]
where the time goes in v4:
time: 149 us
  Pallas kernels  143 us (96%)
  local copies, waits for them, and re-layouts  5.25 us (4%)
    pallas_call x1, Pallas kernels, on_device(): pl.pallas_call(kernel, out_shape=(jax.ShapeDtypeStruct((HALF, O * V), BF1...  143 us

profile of v4, /device:TPU:0, one launch (start us, length us, event | category | flops | bytes accessed | tf_op | source)
XLA Modules:
  0.0 148.6 jit_solution(14189848408776281357)
XLA Ops:
  0.6 1.0 copy.11
  1.6 0.8 reshape.9.w_hbm
  2.5 142.7 %sigma_step.1 = (bf16[24,18432]{1,0:T(8,128)(2,1)}, f32[8,128]{1,0:T(8,128)}) custom-call(bf16[24,18432]{1,0:T(8,128)(2,1)} %r_hbm.1, bf16[24,18432]{1,0:T(8,128)(2,1)} %prev_hbm.1, bf16[2304,1152]{1,0:T(8,128)(2,1)} %c_hbm.1, bf16[144,288]{1,0:T(8,128)(2,1)} %reshape.9.w_hbm, f32[384]{0:T(512)} %vir_ref.1, f32[48]{0:T(128)} %occ_ref.1, f32[64]{0:T(128)} %bprev_ref.1), custom_call_target="tpu_custom_call" | custom-call | tf_op jit(solution)/shard_map/sigma_step/pallas_call | solution.py:519
  145.2 1.3 slice_bitcast_fusion
  146.4 2.1 %copy.13 = bf16[24,18432]{1,0:T(8,128)(2,1)} copy(bf16[24,18432]{1,0:T(8,128)(2,1)} %get-tuple-element.12) | data formatting | bytes 1769472

commit v5 on v4

--- a/solution.py
+++ b/solution.py
@@ -131,9 +131,8 @@
     barrier = pltpu.get_barrier_semaphore()
     for d in range(1, 8):
         pl.semaphore_signal(barrier, inc=1, device_id=((row + d) % 8, col), device_id_type=MESH)
-    for d in range(1, 16):
-        pl.semaphore_signal(barrier, inc=1, device_id=(row, (col + d) % 16), device_id_type=MESH)
-    pl.semaphore_signal(barrier, inc=1, device_id=dev(xl_=1 - xl, xh_=1 - xh), device_id_type=MESH)
+    for to in (sibling, up, down, across):
+        pl.semaphore_signal(barrier, inc=1, device_id=to, device_id_type=MESH)
     load_r = pltpu.make_async_copy(r_hbm, r_ref, load_sem.at[2])
     load_w = pltpu.make_async_copy(w_hbm, w_ref, load_sem.at[3])
     load_r.start()
@@ -143,7 +142,7 @@
     load_p.start()
     load_w.start()
     load_r.wait()
-    pl.semaphore_wait(barrier, 23)
+    pl.semaphore_wait(barrier, 11)
 
     def rel(d):
         yd, xd = (y + d % 4) % 4, (xl + d // 4) % 2

time: 149 us -> 147 us (0.987)
  Pallas kernels: 143 us -> 141 us
    pallas_call x1, Pallas kernels: 143 us -> 141 us  [on_device(): pl.pallas_call(kernel, out_shape=(jax.ShapeDtypeStruct((HALF, O * V), BF1...]
where the time goes in v5:
time: 147 us
  Pallas kernels  141 us (96%)
  local copies, waits for them, and re-layouts  5.25 us (4%)
    pallas_call x1, Pallas kernels, on_device(): pl.pallas_call(kernel, out_shape=(jax.ShapeDtypeStruct((HALF, O * V), BF1...  141 us

profile of v5, /device:TPU:0, one launch (start us, length us, event | category | flops | bytes accessed | tf_op | source)
XLA Modules:
  0.0 146.7 jit_solution(15970468028567612998)
XLA Ops:
  0.6 1.0 copy.11
  1.6 0.8 reshape.9.w_hbm
  2.5 140.8 %sigma_step.1 = (bf16[24,18432]{1,0:T(8,128)(2,1)}, f32[8,128]{1,0:T(8,128)}) custom-call(bf16[24,18432]{1,0:T(8,128)(2,1)} %r_hbm.1, bf16[24,18432]{1,0:T(8,128)(2,1)} %prev_hbm.1, bf16[2304,1152]{1,0:T(8,128)(2,1)} %c_hbm.1, bf16[144,288]{1,0:T(8,128)(2,1)} %reshape.9.w_hbm, f32[384]{0:T(512)} %vir_ref.1, f32[48]{0:T(128)} %occ_ref.1, f32[64]{0:T(128)} %bprev_ref.1), custom_call_target="tpu_custom_call" | custom-call | tf_op jit(solution)/shard_map/sigma_step/pallas_call | solution.py:518
  143.3 1.3 slice_bitcast_fusion
  144.6 2.1 %copy.13 = bf16[24,18432]{1,0:T(8,128)(2,1)} copy(bf16[24,18432]{1,0:T(8,128)(2,1)} %get-tuple-element.12) | data formatting | bytes 1769472
